TPU v7x, 32 devices: a whole 2x2x4 slice. The times are simulated.
32 devices in a mesh: gx: 4 (over y, x), gy: 8 (over z, core).
Axes of the slice: x: 2, y: 2, z: 4, core: 2. Of those that a mesh axis runs over, the one named last changes fastest.
Arguments:
- links: float32 [4, 3, 3, 2, 8, 16, 6, 128], P(None, None, None, None, 'gx', 'gy'), may hold values from -1 to 1, as said below
- incoming: float32 [4, 3, 3, 2, 8, 16, 4, 128], P(None, None, None, None, 'gx', 'gy'), may hold values from -6 to 6
Outputs:
- force: float32 [4, 3, 3, 2, 8, 16, 4, 128], P(None, None, None, None, 'gx', 'gy')
Inputs may be any that keep to these rules, and one draw needn't show every extreme that they name: `links`: each link is a special unitary 3 x 3 matrix.
All inputs are finite; a program needn't handle non-finite values.
Results may differ from a plain program's by a relative error of at most 0.0003.
Values sent between devices are 32-bit elements; how exact they have to be, the bound alone decides.
A program may use at most 128 MiB of HBM per device.

v0:
```python
from functools import partial

import jax
import jax.numpy as jnp
from jax import lax
from jax.experimental import pallas as pl
from jax.experimental.pallas import tpu as pltpu
from jax.sharding import PartitionSpec as P

smear_weight = 0.2
MESH = pl.DeviceIdType.MESH
AXX, AXY, AXZ, AXT = 0, 1, 2, 3
SENT = 12
COMP = 18
ALG = 8
YSLOT = (1, 0, 2, 3)


def re(i, j):
    return (i * 3 + j) * 2


def cmul(a, b):
    return (a[0] * b[0] - a[1] * b[1], a[0] * b[1] + a[1] * b[0])


def cadd(a, b):
    return (a[0] + b[0], a[1] + b[1])


def conj(a):
    return (a[0], -a[1])


def row_times(row, mat, adj=False, acc=None):
    out = []
    for k in range(3):
        total_r = None if acc is None else acc[k][0]
        total_i = None if acc is None else acc[k][1]
        for j in range(3):
            b = mat(k, j) if adj else mat(j, k)
            a = row[j]
            if adj:
                r = a[0] * b[0] + a[1] * b[1]
                i = a[1] * b[0] - a[0] * b[1]
            else:
                r = a[0] * b[0] - a[1] * b[1]
                i = a[0] * b[1] + a[1] * b[0]
            total_r = r if total_r is None else total_r + r
            total_i = i if total_i is None else total_i + i
        out.append((total_r, total_i))
    return out


def getter(load):
    return lambda i, j: (load(re(i, j)), load(re(i, j) + 1))


def row_of(mat, i):
    return [mat(i, j) for j in range(3)]


def adj_row(mat, i):
    return [conj(mat(j, i)) for j in range(3)]


def full(mat):
    values = [[mat(i, j) for j in range(3)] for i in range(3)]
    return lambda i, j: values[i][j]


def of_rows(rows):
    return lambda i, j: rows[i][j]


def traceless_anti(mat):
    diag = [mat(i, i)[1] for i in range(3)]
    third = (diag[0] + diag[1] + diag[2]) * (1.0 / 3.0)
    diag = [v - third for v in diag]
    zero = jnp.zeros_like(third)
    rows = [[None] * 3 for _ in range(3)]
    for i in range(3):
        rows[i][i] = (zero, diag[i])
        for j in range(i + 1, 3):
            a, b = mat(i, j), mat(j, i)
            up = (0.5 * (a[0] - b[0]), 0.5 * (a[1] + b[1]))
            rows[i][j] = up
            rows[j][i] = (-up[0], up[1])
    return of_rows(rows)


def alg_values(mat):
    out = [mat(0, 0)[1], mat(1, 1)[1]]
    for i, j in ((0, 1), (0, 2), (1, 2)):
        out += list(mat(i, j))
    return out


def alg_matrix(load):
    v = [load(k) for k in range(ALG)]
    zero = jnp.zeros_like(v[0])
    rows = [[None] * 3 for _ in range(3)]
    rows[0][0], rows[1][1], rows[2][2] = (zero, v[0]), (zero, v[1]), (zero, -(v[0] + v[1]))
    for k, (i, j) in enumerate(((0, 1), (0, 2), (1, 2))):
        up = (v[2 + 2 * k], v[3 + 2 * k])
        rows[i][j] = up
        rows[j][i] = (-up[0], up[1])
    return of_rows(rows)


def third_row(load, store):
    g = getter(load)
    a, b = row_of(g, 0), row_of(g, 1)
    for k in range(3):
        p, q = (k + 1) % 3, (k + 2) % 3
        u, v = cmul(a[p], b[q]), cmul(a[q], b[p])
        store(re(2, k), u[0] - v[0])
        store(re(2, k) + 1, v[1] - u[1])


def kernel(
    sizes, links, inc, out,
    own, plus, minus, diag, gown, gplus, gminus, gdiag,
    sig, cst, lam,
    hxm, hxp, hym, hyp, cxy, cyx,
    bx5s, bx0s, by5s, by0s, bx5, bx0, by5, by0,
    yup, ydn, lyup, lydn,
    lxm, lxp, lym, lyp, lcxy, lcyx,
    gxm, gxp, gym, gyp, gcxy, gcyx,
    send_sem, recv_sem,
):
    nx, ny = sizes
    wx, wy = links.shape[2], links.shape[3]
    ts = links.shape[4] - 2
    rows, lanes = wy * ts, links.shape[5]
    mx, my = lax.axis_index("gx"), lax.axis_index("gy")
    xu, xd = lax.rem(mx + 1, nx), lax.rem(mx + nx - 1, nx)
    yu, yd = lax.rem(my + 1, ny), lax.rem(my + ny - 1, ny)
    peers = ((xu, my), (xd, my), (mx, yu), (mx, yd), (xu, yd), (xd, yu))

    barrier = pltpu.get_barrier_semaphore()
    for peer in peers:
        pl.semaphore_signal(barrier, inc=1, device_id=peer, device_id_type=MESH)

    row_id = lax.broadcasted_iota(jnp.int32, (rows, lanes), 0)
    t_id = lax.rem(row_id, ts)

    def sub(v, shift):
        shift = shift % rows
        return v if shift == 0 else pltpu.roll(v, shift, 0)

    def lane(v, shift):
        return pltpu.roll(v, shift % lanes, 1)

    def compact(c, _):
        for d in range(4):
            for x in range(wx):
                for y in range(wy):
                    own[d, c, x, y * ts:(y + 1) * ts, :] = links[d, c, x, y, 1:1 + ts, :]
        return 0

    def pack(c, _):
        for d in range(4):
            for x in range(wx):
                yup[YSLOT[d], c, x * ts:(x + 1) * ts, :] = links[d, c, x, wy - 1, 1:1 + ts, :]
                ydn[YSLOT[d], c, x * ts:(x + 1) * ts, :] = links[d, c, x, 0, 1:1 + ts, :]
        for y in range(wy):
            bx5s[c, y:y + 1, :] = links[AXX, c, wx - 1, y, ts + 1:ts + 2, :]
            bx0s[c, y:y + 1, :] = links[AXT, c, 0, y, 0:1, :]
        for x in range(wx):
            by5s[c, x:x + 1, :] = links[AXY, c, x, wy - 1, ts + 1:ts + 2, :]
            by0s[c, x:x + 1, :] = links[AXT, c, x, 0, 0:1, :]
        return 0

    lax.fori_loop(0, COMP, compact, 0)
    lax.fori_loop(0, SENT, pack, 0)
    pl.semaphore_wait(barrier, len(peers))

    def exchange(items, base):
        copies = []
        for k, (src, dst, peer) in enumerate(items):
            copy = pltpu.make_async_remote_copy(
                src_ref=src, dst_ref=dst, send_sem=send_sem.at[base + k],
                recv_sem=recv_sem.at[base + k], device_id=peer, device_id_type=MESH)
            copy.start()
            copies.append(copy)
        return copies

    s = pl.ds(0, SENT)
    first = exchange((
        (own.at[:, s, wx - 1], hxm.at[:, s], peers[0]),
        (own.at[1:4, s, 0], hxp.at[1:4, s], peers[1]),
        (yup, hym.at[:, s], peers[2]),
        (ydn.at[1:4], hyp.at[1:4, s], peers[3]),
        (own.at[AXX, s, wx - 1], cxy.at[s], peers[4]),
        (own.at[AXY, s, 0], cyx.at[s], peers[5]),
        (bx5s, bx5.at[s], peers[0]),
        (bx0s, bx0.at[s], peers[1]),
        (by5s, by5.at[s], peers[2]),
        (by0s, by0.at[s], peers[3]),
    ), 0)

    def compact_in(c, _):
        for d in range(4):
            for x in range(wx):
                for y in range(wy):
                    sig[d, c, x, y * ts:(y + 1) * ts, :] = inc[d, c, x, y]
        return 0

    lax.fori_loop(0, COMP, compact_in, 0)
    for copy in first:
        copy.wait()

    def fix(ref, *index):
        def store(c, v):
            ref[(*index, c)] = v
        third_row(lambda c: ref[(*index, c)], store)

    def fix_four(d, _):
        fix(hxm, d)
        fix(hym, d)
        return 0

    def fix_three(d, _):
        fix(hxp, d)
        fix(hyp, d)
        return 0

    lax.fori_loop(0, 4, fix_four, 0)
    lax.fori_loop(1, 4, fix_three, 0)
    for ref in (cxy, cyx, bx5, bx0, by5, by0):
        fix(ref)

    def spread(parts):
        v = jnp.broadcast_to(parts[-1], (rows, lanes))
        for y in range(wy - 2, -1, -1):
            v = jnp.where(row_id < (y + 1) * ts, jnp.broadcast_to(parts[y], (rows, lanes)), v)
        return v

    def t_ahead(v, parts):
        edge = 0.0 if parts is None else spread(parts)
        return jnp.where(t_id == ts - 1, edge, sub(v, -1))

    def t_behind(v, parts):
        edge = 0.0 if parts is None else spread(parts)
        return jnp.where(t_id == 0, edge, sub(v, 1))

    def y_ahead(v, halo, x):
        return jnp.where(row_id >= (wy - 1) * ts, sub(halo, (wy - 1 - x) * ts), sub(v, -ts))

    def y_behind(v, halo, x):
        return jnp.where(row_id < ts, sub(halo, -x * ts), sub(v, ts))

    def build(own, plus, minus, diag, hxm, hxp, hym, hyp, cxy, cyx, edges):
        def low(d, c, x):
            return [links[d, c, x, y, 0:1, :] for y in range(wy)] if edges else None

        def high(d, c, x):
            return [links[d, c, x, y, ts + 1:ts + 2, :] for y in range(wy)] if edges else None

        def pick(ref, c, n):
            return [ref[c, k:k + 1, :] for k in range(n)] if edges else None

        def body(c, _):
            for x in range(wx):
                for d in range(4):
                    here = own[d, c, x]
                    if d != AXX:
                        plus[d, AXX, c, x] = own[d, c, x + 1] if x + 1 < wx else hxp[d, c]
                    if d != AXY:
                        plus[d, AXY, c, x] = y_ahead(here, hyp[YSLOT[d], c], x)
                    if d != AXZ:
                        plus[d, AXZ, c, x] = lane(here, -1)
                    if d != AXT:
                        plus[d, AXT, c, x] = t_ahead(here, high(d, c, x))
                    minus[d, AXX, c, x] = own[d, c, x - 1] if x > 0 else hxm[d, c]
                    minus[d, AXY, c, x] = y_behind(here, hym[YSLOT[d], c], x)
                    minus[d, AXZ, c, x] = lane(here, 1)
                    minus[d, AXT, c, x] = t_behind(here, low(d, c, x))
            for x in range(wx):
                last = x + 1 == wx
                if x == 0:
                    edge = hxm[AXX, c]
                    diag[AXX, AXY, c, x] = jnp.where(
                        row_id >= (wy - 1) * ts, sub(cxy[c], (wy - 1) * ts), sub(edge, -ts))
                    diag[AXX, AXZ, c, x] = lane(edge, -1)
                    diag[AXX, AXT, c, x] = t_ahead(edge, pick(bx5, c, wy))
                else:
                    for m in (AXY, AXZ, AXT):
                        diag[AXX, m, c, x] = plus[AXX, m, c, x - 1]
                back = minus[AXY, AXY, c, x]
                if last:
                    diag[AXY, AXX, c, x] = jnp.where(
                        row_id < ts, sub(cyx[c], -(wy - 1) * ts), sub(hxp[AXY, c], ts))
                else:
                    diag[AXY, AXX, c, x] = minus[AXY, AXY, c, x + 1]
                diag[AXY, AXZ, c, x] = lane(back, -1)
                parts = None
                if edges:
                    parts = [by5[c, x:x + 1, :]] + high(AXY, c, x)[:wy - 1]
                diag[AXY, AXT, c, x] = t_ahead(back, parts)
                diag[AXZ, AXX, c, x] = lane(hxp[AXZ, c], 1) if last else minus[AXZ, AXZ, c, x + 1]
                diag[AXZ, AXY, c, x] = lane(plus[AXZ, AXY, c, x], 1)
                diag[AXZ, AXT, c, x] = lane(plus[AXZ, AXT, c, x], 1)
                if last:
                    diag[AXT, AXX, c, x] = t_behind(hxp[AXT, c], pick(bx0, c, wy))
                else:
                    diag[AXT, AXX, c, x] = minus[AXT, AXT, c, x + 1]
                parts = None
                if edges:
                    parts = low(AXT, c, x)[1:] + [by0[c, x:x + 1, :]]
                diag[AXT, AXY, c, x] = t_behind(plus[AXT, AXY, c, x], parts)
                diag[AXT, AXZ, c, x] = lane(minus[AXT, AXT, c, x], -1)
            return 0

        lax.fori_loop(0, COMP, body, 0)

    build(own, plus, minus, diag, hxm, hxp, hym, hyp, cxy, cyx, True)

    def link(ref, *index):
        return getter(lambda c: ref[(*index[:-1], c, index[-1])])

    def site(q, _):
        m, x = q // wx, lax.rem(q, wx)
        c_rows = [None] * 3
        for k in range(1, 4):
            n = lax.rem(m + k, 4)
            n_own, m_ahead, n_ahead = link(own, n, x), link(plus, m, n, x), link(plus, n, m, x)
            n_back, m_back, n_diag = link(minus, n, n, x), link(minus, m, n, x), link(diag, n, m, x)
            for i in range(3):
                part = row_times(row_of(n_own, i), m_ahead)
                c_rows[i] = row_times(part, n_ahead, adj=True, acc=c_rows[i])
                part = row_times(adj_row(n_back, i), m_back)
                c_rows[i] = row_times(part, n_diag, acc=c_rows[i])
        for i in range(3):
            for j in range(3):
                v = c_rows[i][j]
                cst[m, re(i, j), x] = smear_weight * v[0]
                cst[m, re(i, j) + 1, x] = smear_weight * v[1]
        return 0

    lax.fori_loop(0, 4 * wx, site, 0)

    def algebra(q, _):
        m, x = q // wx, lax.rem(q, wx)
        u, staple, target = link(own, m, x), link(cst, m, x), link(sig, m, x)
        omega = of_rows([row_times(row_of(staple, i), u, adj=True) for i in range(3)])
        a = traceless_anti(omega)
        a2 = of_rows([row_times(row_of(a, i), a) for i in range(3)])
        p = 0.5 * (a2(0, 0)[0] + a2(1, 1)[0] + a2(2, 2)[0])
        det = None
        for i in range(3):
            for j in range(3):
                v = cmul(a2(i, j), a(j, i))[1]
                det = v if det is None else det + v
        det = det * (1.0 / 3.0)
        f0 = (1.0 - det * det * (1.0 / 720), det * (1.0 / 6 + p * (1.0 / 120)))
        f1 = (1.0 + p * (1.0 / 6 + p * (1.0 / 120)), det * (1.0 / 24 + p * (1.0 / 360)))
        f2 = (0.5 + p * (1.0 / 24 + p * (1.0 / 720)), det * (1.0 / 120))
        e = []
        for i in range(3):
            e.append([])
            for j in range(3):
                v = cadd(cmul(f1, a(i, j)), cmul(f2, a2(i, j)))
                e[i].append(cadd(v, f0) if i == j else v)
        e = of_rows(e)
        direct = [row_times(adj_row(e, i), target) for i in range(3)]
        cot = of_rows([row_times(row_of(target, i), u, adj=True) for i in range(3)])
        t0 = (cot(0, 0)[0] + cot(1, 1)[0] + cot(2, 2)[0], -(cot(0, 0)[1] + cot(1, 1)[1] + cot(2, 2)[1]))
        t1, t2 = None, None
        for i in range(3):
            for j in range(3):
                g = conj(cot(i, j))
                v1, v2 = cmul(g, a(i, j)), cmul(g, a2(i, j))
                t1 = v1 if t1 is None else cadd(t1, v1)
                t2 = v2 if t2 is None else cadd(t2, v2)
        p_bar = (-t0[1] * det * (1.0 / 120) + t1[0] * (1.0 / 6 + p * (1.0 / 60))
                 - t1[1] * det * (1.0 / 360) + t2[0] * (1.0 / 24 + p * (1.0 / 360)))
        d_bar = (-t0[0] * det * (1.0 / 360) - t0[1] * (1.0 / 6 + p * (1.0 / 120))
                 - t1[1] * (1.0 / 24 + p * (1.0 / 360)) - t2[1] * (1.0 / 120))
        both = []
        for i in range(3):
            v = row_times(row_of(a, i), cot)
            both.append(row_times(row_of(cot, i), a, acc=v))
        bar = []
        g1, g2 = conj(f1), conj(f2)
        for i in range(3):
            bar.append([])
            for j in range(3):
                v1, v2 = cmul(g1, cot(i, j)), cmul(g2, both[i][j])
                aa, aq = a(i, j), a2(i, j)
                bar[i].append((v1[0] - v2[0] - p_bar * aa[0] - d_bar * aq[1],
                               v1[1] - v2[1] - p_bar * aa[1] + d_bar * aq[0]))
        alg = traceless_anti(of_rows(bar))
        for k, v in enumerate(alg_values(alg)):
            lam[m, k, x] = v
        less = [row_times(row_of(alg, i), staple) for i in range(3)]
        for i in range(3):
            for j in range(3):
                cst[m, re(i, j), x] = direct[i][j][0] - less[i][j][0]
                cst[m, re(i, j) + 1, x] = direct[i][j][1] - less[i][j][1]
        return 0

    lax.fori_loop(0, 4 * wx, algebra, 0)

    def pack_alg(k, _):
        for d in range(4):
            for x in range(wx):
                v = lam[d, k, x]
                lyup[YSLOT[d], k, x * ts:(x + 1) * ts, :] = v[(wy - 1) * ts:, :]
                lydn[YSLOT[d], k, x * ts:(x + 1) * ts, :] = v[:ts, :]
        return 0

    lax.fori_loop(0, ALG, pack_alg, 0)
    second = exchange((
        (lam.at[:, :, wx - 1], lxm, peers[0]),
        (lam.at[1:4, :, 0], lxp.at[1:4], peers[1]),
        (lyup, lym, peers[2]),
        (lydn.at[1:4], lyp.at[1:4], peers[3]),
        (lam.at[AXX, :, wx - 1], lcxy, peers[4]),
        (lam.at[AXY, :, 0], lcyx, peers[5]),
    ), len(first))

    def widen(load_alg, load_link, store):
        alg = alg_matrix(lambda k: smear_weight * load_alg(k))
        u = getter(load_link)
        for i in range(3):
            v = row_times(row_of(alg, i), u)
            for j in range(3):
                store(re(i, j), v[j][0])
                store(re(i, j) + 1, v[j][1])

    def widen_own(q, _):
        m, x = q // wx, lax.rem(q, wx)

        def store(c, v):
            gown[m, c, x] = v
        widen(lambda k: lam[m, k, x], lambda c: own[m, c, x], store)
        return 0

    lax.fori_loop(0, 4 * wx, widen_own, 0)
    for copy in second:
        copy.wait()

    def widen_halo(alg, ref, dst, *index):
        def store(c, v):
            dst[(*index, c)] = v
        widen(lambda k: alg[(*index, k)], lambda c: ref[(*index, c)], store)

    def widen_four(d, _):
        widen_halo(lxm, hxm, gxm, d)
        widen_halo(lym, hym, gym, d)
        return 0

    def widen_three(d, _):
        widen_halo(lxp, hxp, gxp, d)
        widen_halo(lyp, hyp, gyp, d)
        return 0

    lax.fori_loop(0, 4, widen_four, 0)
    lax.fori_loop(1, 4, widen_three, 0)
    widen_halo(lcxy, cxy, gcxy)
    widen_halo(lcyx, cyx, gcyx)

    build(gown, gplus, gminus, gdiag, gxm, gxp, gym, gyp, gcxy, gcyx, False)

    def force(q, _):
        m, x = q // wx, lax.rem(q, wx)
        base = link(cst, m, x)
        rows_out = [row_of(base, i) for i in range(3)]
        for k in range(1, 4):
            n = lax.rem(m + k, 4)
            n_own, m_ahead, n_ahead = link(own, n, x), link(plus, m, n, x), link(plus, n, m, x)
            n_back, m_back, n_diag = link(minus, n, n, x), link(minus, m, n, x), link(diag, n, m, x)
            gn_own, gm_ahead, gn_ahead = link(gown, n, x), link(gplus, m, n, x), link(gplus, n, m, x)
            gn_back, gm_back, gn_diag = link(gminus, n, n, x), link(gminus, m, n, x), link(gdiag, n, m, x)
            for i in range(3):
                u_row = row_of(n_own, i)
                v = row_times(u_row, gm_ahead)
                v = row_times(row_of(gn_own, i), m_ahead, acc=v)
                acc = row_times(v, n_ahead, adj=True, acc=rows_out[i])
                v = row_times(u_row, m_ahead)
                acc = row_times(v, gn_ahead, adj=True, acc=acc)
                u_row = adj_row(n_back, i)
                v = row_times(u_row, gm_back)
                v = row_times(adj_row(gn_back, i), m_back, acc=v)
                acc = row_times(v, n_diag, acc=acc)
                v = row_times(u_row, m_back)
                rows_out[i] = row_times(v, gn_diag, acc=acc)
        for i in range(3):
            for j in range(3):
                for part in range(2):
                    v = rows_out[i][j][part]
                    for y in range(wy):
                        out[m, re(i, j) + part, x, y] = v[y * ts:(y + 1) * ts, :]
        return 0

    lax.fori_loop(0, 4 * wx, force, 0)


def solution(mesh):
    sizes = (mesh.shape["gx"], mesh.shape["gy"])

    def body(links, incoming):
        dirs, _, _, _, wx, wy, _, lanes = links.shape
        ts = incoming.shape[6]
        rows = wy * ts
        flat = links.reshape(dirs, COMP, *links.shape[4:])
        flat_in = incoming.reshape(dirs, COMP, *incoming.shape[4:])
        f32 = jnp.float32

        def vm(*shape):
            return pltpu.VMEM((*shape, lanes), f32)

        field = vm(dirs, COMP, wx, rows)
        pairs = vm(dirs, dirs, COMP, wx, rows)
        halo = vm(dirs, COMP, rows)
        corner = vm(COMP, rows)
        scratch = [field, pairs, pairs, pairs, field, pairs, pairs, pairs]
        scratch += [field, field, vm(dirs, ALG, wx, rows)]
        scratch += [halo] * 4 + [corner] * 2
        scratch += [vm(SENT, wy)] * 2 + [vm(SENT, wx)] * 2 + [vm(COMP, wy)] * 2 + [vm(COMP, wx)] * 2
        scratch += [vm(dirs, SENT, rows)] * 2 + [vm(dirs, ALG, rows)] * 2
        scratch += [vm(dirs, ALG, rows)] * 4 + [vm(ALG, rows)] * 2
        scratch += [halo] * 4 + [corner] * 2
        scratch += [pltpu.SemaphoreType.DMA((16,)), pltpu.SemaphoreType.DMA((16,))]
        result = pl.pallas_call(
            partial(kernel, sizes),
            out_shape=jax.ShapeDtypeStruct(flat_in.shape, f32),
            in_specs=[pl.BlockSpec(memory_space=pltpu.VMEM)] * 2,
            out_specs=pl.BlockSpec(memory_space=pltpu.VMEM),
            scratch_shapes=scratch,
            compiler_params=pltpu.CompilerParams(
                collective_id=0, has_side_effects=True, vmem_limit_bytes=60 << 20),
            name="stout",
        )(flat, flat_in)
        return result.reshape(incoming.shape)

    placed = P(None, None, None, None, "gx", "gy", None, None)
    return jax.shard_map(
        body, mesh=mesh, in_specs=(placed, placed), out_specs=placed, check_vma=False)
```

profile of v0, /device:TPU:0, one launch (start us, length us, event | category | flops | bytes accessed | tf_op | source)
XLA Modules:
  0.0 48.9 jit_solution(170107177818420949)
XLA Ops:
  0.0 2.3 %copy.3 = f32[4,3,3,2,2,2,6,128]{7,6,5,4,3,2,1,0:T(8,128)} copy(f32[4,3,3,2,2,2,6,128]{7,5,6,4,3,2,1,0:T(2,128)} %param.2) | data formatting | bytes 1769472 | tf_op args[0]
  2.4 44.6 %stout.1 = f32[4,18,2,2,4,128]{5,4,3,2,1,0:T(4,128)} custom-call(f32[4,18,2,2,6,128]{5,4,3,2,1,0:T(8,128)} %bitcast.3, f32[4,18,2,2,4,128]{5,4,3,2,1,0:T(4,128)} %bitcast.5), custom_call_target="tpu_custom_call" | custom-call | tf_op jit(solution)/shard_map/stout/pallas_call | solution.py:527
  46.9 2.0 %copy.5 = f32[4,3,3,2,2,2,4,128]{7,6,5,4,3,2,1,0:T(4,128)} copy(f32[4,3,3,2,2,2,4,128]{7,6,5,4,3,2,1,0:T(4,128)} %bitcast.4) | data formatting | bytes 1179648
where the time goes:
time: 49.1 us; the launch traced here: 48.9 us
  Pallas kernels  44.6 us (91%)
  local copies, waits for them, and re-layouts  4.3 us (9%)
    pallas_call x1, Pallas kernels, body(): pl.pallas_call(partial(kernel, sizes), out_shape=jax.ShapeDtypeStruct(fla...  44.6 us
    unnamed x2, local copies, waits for them, and re-layouts  4.3 us

commit v1 on v0

--- a/solution.py
+++ b/solution.py
@@ -123,7 +123,7 @@
     own, plus, minus, diag, gown, gplus, gminus, gdiag,
     sig, cst, lam,
     hxm, hxp, hym, hyp, cxy, cyx,
-    bx5s, bx0s, by5s, by0s, bx5, bx0, by5, by0,
+    cxs, cys, lcxs, lcys, bx5s, bx0s, by5s, by0s, bx5, bx0, by5, by0,
     yup, ydn, lyup, lydn,
     lxm, lxp, lym, lyp, lcxy, lcyx,
     gxm, gxp, gym, gyp, gcxy, gcyx,
@@ -152,6 +152,9 @@
     def lane(v, shift):
         return pltpu.roll(v, shift % lanes, 1)
 
+    def tiled(v):
+        return jnp.concatenate([v] * wy, axis=0)
+
     def compact(c, _):
         for d in range(4):
             for x in range(wx):
@@ -164,6 +167,8 @@
             for x in range(wx):
                 yup[YSLOT[d], c, x * ts:(x + 1) * ts, :] = links[d, c, x, wy - 1, 1:1 + ts, :]
                 ydn[YSLOT[d], c, x * ts:(x + 1) * ts, :] = links[d, c, x, 0, 1:1 + ts, :]
+        cxs[c] = links[AXX, c, wx - 1, 0, 1:1 + ts, :]
+        cys[c] = links[AXY, c, 0, wy - 1, 1:1 + ts, :]
         for y in range(wy):
             bx5s[c, y:y + 1, :] = links[AXX, c, wx - 1, y, ts + 1:ts + 2, :]
             bx0s[c, y:y + 1, :] = links[AXT, c, 0, y, 0:1, :]
@@ -192,8 +197,8 @@
         (own.at[1:4, s, 0], hxp.at[1:4, s], peers[1]),
         (yup, hym.at[:, s], peers[2]),
         (ydn.at[1:4], hyp.at[1:4, s], peers[3]),
-        (own.at[AXX, s, wx - 1], cxy.at[s], peers[4]),
-        (own.at[AXY, s, 0], cyx.at[s], peers[5]),
+        (cxs, cxy.at[s], peers[4]),
+        (cys, cyx.at[s], peers[5]),
         (bx5s, bx5.at[s], peers[0]),
         (bx0s, bx0.at[s], peers[1]),
         (by5s, by5.at[s], peers[2]),
@@ -205,31 +210,42 @@
             for x in range(wx):
                 for y in range(wy):
                     sig[d, c, x, y * ts:(y + 1) * ts, :] = inc[d, c, x, y]
+                cst[d, c, x] = jnp.zeros((rows, lanes), jnp.float32)
         return 0
 
     lax.fori_loop(0, COMP, compact_in, 0)
-    for copy in first:
-        copy.wait()
-
     def fix(ref, *index):
         def store(c, v):
             ref[(*index, c)] = v
         third_row(lambda c: ref[(*index, c)], store)
 
-    def fix_four(d, _):
-        fix(hxm, d)
-        fix(hym, d)
-        return 0
-
-    def fix_three(d, _):
-        fix(hxp, d)
-        fix(hyp, d)
-        return 0
-
-    lax.fori_loop(0, 4, fix_four, 0)
-    lax.fori_loop(1, 4, fix_three, 0)
-    for ref in (cxy, cyx, bx5, bx0, by5, by0):
-        fix(ref)
+    def fix_y():
+        def four(d, _):
+            fix(hym, d)
+            return 0
+
+        def three(d, _):
+            fix(hyp, d)
+            return 0
+
+        lax.fori_loop(0, 4, four, 0)
+        lax.fori_loop(1, 4, three, 0)
+        for ref in (by5, by0):
+            fix(ref)
+
+    def fix_x():
+        def four(d, _):
+            fix(hxm, d)
+            return 0
+
+        def three(d, _):
+            fix(hxp, d)
+            return 0
+
+        lax.fori_loop(0, 4, four, 0)
+        lax.fori_loop(1, 4, three, 0)
+        for ref in (cxy, cyx, bx5, bx0):
+            fix(ref)
 
     def spread(parts):
         v = jnp.broadcast_to(parts[-1], (rows, lanes))
@@ -251,7 +267,7 @@
     def y_behind(v, halo, x):
         return jnp.where(row_id < ts, sub(halo, -x * ts), sub(v, ts))
 
-    def build(own, plus, minus, diag, hxm, hxp, hym, hyp, cxy, cyx, edges):
+    def build(own, plus, minus, diag, hxm, hxp, hym, hyp, cxy, cyx, edges, stage):
         def low(d, c, x):
             return [links[d, c, x, y, 0:1, :] for y in range(wy)] if edges else None
 
@@ -265,85 +281,106 @@
             for x in range(wx):
                 for d in range(4):
                     here = own[d, c, x]
-                    if d != AXX:
-                        plus[d, AXX, c, x] = own[d, c, x + 1] if x + 1 < wx else hxp[d, c]
-                    if d != AXY:
-                        plus[d, AXY, c, x] = y_ahead(here, hyp[YSLOT[d], c], x)
-                    if d != AXZ:
-                        plus[d, AXZ, c, x] = lane(here, -1)
-                    if d != AXT:
-                        plus[d, AXT, c, x] = t_ahead(here, high(d, c, x))
-                    minus[d, AXX, c, x] = own[d, c, x - 1] if x > 0 else hxm[d, c]
-                    minus[d, AXY, c, x] = y_behind(here, hym[YSLOT[d], c], x)
-                    minus[d, AXZ, c, x] = lane(here, 1)
-                    minus[d, AXT, c, x] = t_behind(here, low(d, c, x))
+                    if stage == 0:
+                        if d != AXX:
+                            plus[d, AXX, c, x] = own[d, c, x + 1] if x + 1 < wx else hxp[d, c]
+                        minus[d, AXX, c, x] = own[d, c, x - 1] if x > 0 else hxm[d, c]
+                    if stage == 1:
+                        if d != AXY:
+                            plus[d, AXY, c, x] = y_ahead(here, hyp[YSLOT[d], c], x)
+                        minus[d, AXY, c, x] = y_behind(here, hym[YSLOT[d], c], x)
+                    if stage == 2:
+                        if d != AXZ:
+                            plus[d, AXZ, c, x] = lane(here, -1)
+                        if d != AXT:
+                            plus[d, AXT, c, x] = t_ahead(here, high(d, c, x))
+                        minus[d, AXZ, c, x] = lane(here, 1)
+                        minus[d, AXT, c, x] = t_behind(here, low(d, c, x))
             for x in range(wx):
                 last = x + 1 == wx
-                if x == 0:
-                    edge = hxm[AXX, c]
-                    diag[AXX, AXY, c, x] = jnp.where(
-                        row_id >= (wy - 1) * ts, sub(cxy[c], (wy - 1) * ts), sub(edge, -ts))
-                    diag[AXX, AXZ, c, x] = lane(edge, -1)
-                    diag[AXX, AXT, c, x] = t_ahead(edge, pick(bx5, c, wy))
-                else:
-                    for m in (AXY, AXZ, AXT):
-                        diag[AXX, m, c, x] = plus[AXX, m, c, x - 1]
-                back = minus[AXY, AXY, c, x]
-                if last:
-                    diag[AXY, AXX, c, x] = jnp.where(
-                        row_id < ts, sub(cyx[c], -(wy - 1) * ts), sub(hxp[AXY, c], ts))
-                else:
-                    diag[AXY, AXX, c, x] = minus[AXY, AXY, c, x + 1]
-                diag[AXY, AXZ, c, x] = lane(back, -1)
-                parts = None
-                if edges:
-                    parts = [by5[c, x:x + 1, :]] + high(AXY, c, x)[:wy - 1]
-                diag[AXY, AXT, c, x] = t_ahead(back, parts)
-                diag[AXZ, AXX, c, x] = lane(hxp[AXZ, c], 1) if last else minus[AXZ, AXZ, c, x + 1]
-                diag[AXZ, AXY, c, x] = lane(plus[AXZ, AXY, c, x], 1)
-                diag[AXZ, AXT, c, x] = lane(plus[AXZ, AXT, c, x], 1)
-                if last:
-                    diag[AXT, AXX, c, x] = t_behind(hxp[AXT, c], pick(bx0, c, wy))
-                else:
-                    diag[AXT, AXX, c, x] = minus[AXT, AXT, c, x + 1]
-                parts = None
-                if edges:
-                    parts = low(AXT, c, x)[1:] + [by0[c, x:x + 1, :]]
-                diag[AXT, AXY, c, x] = t_behind(plus[AXT, AXY, c, x], parts)
-                diag[AXT, AXZ, c, x] = lane(minus[AXT, AXT, c, x], -1)
+                if stage == 2:
+                    diag[AXZ, AXT, c, x] = lane(plus[AXZ, AXT, c, x], 1)
+                    diag[AXT, AXZ, c, x] = lane(minus[AXT, AXT, c, x], -1)
+                if stage == 1:
+                    back = minus[AXY, AXY, c, x]
+                    diag[AXY, AXZ, c, x] = lane(back, -1)
+                    parts = None
+                    if edges:
+                        parts = [by5[c, x:x + 1, :]] + high(AXY, c, x)[:wy - 1]
+                    diag[AXY, AXT, c, x] = t_ahead(back, parts)
+                    diag[AXZ, AXY, c, x] = lane(plus[AXZ, AXY, c, x], 1)
+                    parts = None
+                    if edges:
+                        parts = low(AXT, c, x)[1:] + [by0[c, x:x + 1, :]]
+                    diag[AXT, AXY, c, x] = t_behind(plus[AXT, AXY, c, x], parts)
+                if stage == 0:
+                    if x == 0:
+                        edge = hxm[AXX, c]
+                        diag[AXX, AXY, c, x] = jnp.where(
+                            row_id >= (wy - 1) * ts, tiled(cxy[c]), sub(edge, -ts))
+                        diag[AXX, AXZ, c, x] = lane(edge, -1)
+                        diag[AXX, AXT, c, x] = t_ahead(edge, pick(bx5, c, wy))
+                    else:
+                        for m in (AXY, AXZ, AXT):
+                            diag[AXX, m, c, x] = plus[AXX, m, c, x - 1]
+                    if last:
+                        diag[AXY, AXX, c, x] = jnp.where(
+                            row_id < ts, tiled(cyx[c]), sub(hxp[AXY, c], ts))
+                        diag[AXZ, AXX, c, x] = lane(hxp[AXZ, c], 1)
+                        diag[AXT, AXX, c, x] = t_behind(hxp[AXT, c], pick(bx0, c, wy))
+                    else:
+                        for m in (AXY, AXZ, AXT):
+                            diag[m, AXX, c, x] = minus[m, m, c, x + 1]
             return 0
 
         lax.fori_loop(0, COMP, body, 0)
 
-    build(own, plus, minus, diag, hxm, hxp, hym, hyp, cxy, cyx, True)
+    def build_links(stage):
+        build(own, plus, minus, diag, hxm, hxp, hym, hyp, cxy, cyx, True, stage)
 
     def link(ref, *index):
         return getter(lambda c: ref[(*index[:-1], c, index[-1])])
 
-    def site(q, _):
-        m, x = q // wx, lax.rem(q, wx)
-        c_rows = [None] * 3
-        for k in range(1, 4):
-            n = lax.rem(m + k, 4)
-            n_own, m_ahead, n_ahead = link(own, n, x), link(plus, m, n, x), link(plus, n, m, x)
-            n_back, m_back, n_diag = link(minus, n, n, x), link(minus, m, n, x), link(diag, n, m, x)
-            for i in range(3):
-                part = row_times(row_of(n_own, i), m_ahead)
-                c_rows[i] = row_times(part, n_ahead, adj=True, acc=c_rows[i])
-                part = row_times(adj_row(n_back, i), m_back)
-                c_rows[i] = row_times(part, n_diag, acc=c_rows[i])
-        for i in range(3):
-            for j in range(3):
-                v = c_rows[i][j]
-                cst[m, re(i, j), x] = smear_weight * v[0]
-                cst[m, re(i, j) + 1, x] = smear_weight * v[1]
-        return 0
-
-    lax.fori_loop(0, 4 * wx, site, 0)
-
-    def algebra(q, _):
-        m, x = q // wx, lax.rem(q, wx)
-        u, staple, target = link(own, m, x), link(cst, m, x), link(sig, m, x)
+    def planes(base, work):
+        def step(q, _):
+            pair, x = q // wx, lax.rem(q, wx)
+            gap, swap = 1 + pair // 2, lax.rem(pair, 2)
+            work(base + gap * swap, base + gap * (1 - swap), x)
+            return 0
+
+        lax.fori_loop(0, 2 * (3 - base) * wx, step, 0)
+
+    def put(m, x, i, values):
+        for j in range(3):
+            cst[m, re(i, j), x] = values[j][0]
+            cst[m, re(i, j) + 1, x] = values[j][1]
+
+    def site(m, n, x):
+        n_own, m_ahead, n_ahead = link(own, n, x), link(plus, m, n, x), link(plus, n, m, x)
+        n_back, m_back, n_diag = link(minus, n, n, x), link(minus, m, n, x), link(diag, n, m, x)
+        total = link(cst, m, x)
+        for i in range(3):
+            part = row_times(row_of(n_own, i), m_ahead)
+            acc = row_times(part, n_ahead, adj=True, acc=row_of(total, i))
+            part = row_times(adj_row(n_back, i), m_back)
+            put(m, x, i, row_times(part, n_diag, acc=acc))
+
+    build_links(2)
+    planes(2, site)
+    for k in (2, 3, 8, 9):
+        first[k].wait()
+    fix_y()
+    build_links(1)
+    planes(1, site)
+    for k in (0, 1, 4, 5, 6, 7):
+        first[k].wait()
+    fix_x()
+    build_links(0)
+    planes(0, site)
+
+    def algebra(m, x, _):
+        u, raw, target = link(own, m, x), link(cst, m, x), link(sig, m, x)
+        staple = full(lambda i, j: tuple(smear_weight * v for v in raw(i, j)))
         omega = of_rows([row_times(row_of(staple, i), u, adj=True) for i in range(3)])
         a = traceless_anti(omega)
         a2 = of_rows([row_times(row_of(a, i), a) for i in range(3)])
@@ -401,25 +438,32 @@
                 cst[m, re(i, j) + 1, x] = direct[i][j][1] - less[i][j][1]
         return 0
 
-    lax.fori_loop(0, 4 * wx, algebra, 0)
-
-    def pack_alg(k, _):
-        for d in range(4):
-            for x in range(wx):
-                v = lam[d, k, x]
-                lyup[YSLOT[d], k, x * ts:(x + 1) * ts, :] = v[(wy - 1) * ts:, :]
-                lydn[YSLOT[d], k, x * ts:(x + 1) * ts, :] = v[:ts, :]
-        return 0
-
-    lax.fori_loop(0, ALG, pack_alg, 0)
-    second = exchange((
-        (lam.at[:, :, wx - 1], lxm, peers[0]),
-        (lam.at[1:4, :, 0], lxp.at[1:4], peers[1]),
-        (lyup, lym, peers[2]),
-        (lydn.at[1:4], lyp.at[1:4], peers[3]),
-        (lam.at[AXX, :, wx - 1], lcxy, peers[4]),
-        (lam.at[AXY, :, 0], lcyx, peers[5]),
-    ), len(first))
+    second_x, second_y = [], []
+    for m in range(4):
+        lax.fori_loop(0, wx, partial(algebra, m), 0)
+        slot = YSLOT[m]
+        for k in range(ALG):
+            for x in range(wx):
+                v = lam[m, k, x]
+                lyup[slot, k, x * ts:(x + 1) * ts, :] = v[(wy - 1) * ts:, :]
+                if m != AXY:
+                    lydn[slot, k, x * ts:(x + 1) * ts, :] = v[:ts, :]
+            if m == AXX:
+                lcxs[k] = lam[m, k, wx - 1][:ts, :]
+            if m == AXY:
+                lcys[k] = lam[m, k, 0][(wy - 1) * ts:, :]
+        items = [(lam.at[m, :, wx - 1], lxm.at[m], peers[0])]
+        if m != AXX:
+            items.append((lam.at[m, :, 0], lxp.at[m], peers[1]))
+        if m == AXX:
+            items.append((lcxs, lcxy, peers[4]))
+        if m == AXY:
+            items.append((lcys, lcyx, peers[5]))
+        second_x += exchange(items, len(first) + len(second_x) + len(second_y))
+        items = [(lyup.at[slot], lym.at[slot], peers[2])]
+        if m != AXY:
+            items.append((lydn.at[slot], lyp.at[slot], peers[3]))
+        second_y += exchange(items, len(first) + len(second_x) + len(second_y))
 
     def widen(load_alg, load_link, store):
         alg = alg_matrix(lambda k: smear_weight * load_alg(k))
@@ -439,63 +483,69 @@
         return 0
 
     lax.fori_loop(0, 4 * wx, widen_own, 0)
-    for copy in second:
-        copy.wait()
-
     def widen_halo(alg, ref, dst, *index):
         def store(c, v):
             dst[(*index, c)] = v
         widen(lambda k: alg[(*index, k)], lambda c: ref[(*index, c)], store)
 
-    def widen_four(d, _):
-        widen_halo(lxm, hxm, gxm, d)
-        widen_halo(lym, hym, gym, d)
-        return 0
-
-    def widen_three(d, _):
-        widen_halo(lxp, hxp, gxp, d)
-        widen_halo(lyp, hyp, gyp, d)
-        return 0
-
-    lax.fori_loop(0, 4, widen_four, 0)
-    lax.fori_loop(1, 4, widen_three, 0)
+    def widen_faces(pairs_four, pairs_three):
+        def four(d, _):
+            widen_halo(*pairs_four, d)
+            return 0
+
+        def three(d, _):
+            widen_halo(*pairs_three, d)
+            return 0
+
+        lax.fori_loop(0, 4, four, 0)
+        lax.fori_loop(1, 4, three, 0)
+
+    def build_g(stage):
+        build(gown, gplus, gminus, gdiag, gxm, gxp, gym, gyp, gcxy, gcyx, False, stage)
+
+    def force(m, n, x):
+        n_own, m_ahead, n_ahead = link(own, n, x), link(plus, m, n, x), link(plus, n, m, x)
+        n_back, m_back, n_diag = link(minus, n, n, x), link(minus, m, n, x), link(diag, n, m, x)
+        gn_own, gm_ahead, gn_ahead = link(gown, n, x), link(gplus, m, n, x), link(gplus, n, m, x)
+        gn_back, gm_back, gn_diag = link(gminus, n, n, x), link(gminus, m, n, x), link(gdiag, n, m, x)
+        total = link(cst, m, x)
+        for i in range(3):
+            u_row = row_of(n_own, i)
+            v = row_times(u_row, gm_ahead)
+            v = row_times(row_of(gn_own, i), m_ahead, acc=v)
+            acc = row_times(v, n_ahead, adj=True, acc=row_of(total, i))
+            v = row_times(u_row, m_ahead)
+            acc = row_times(v, gn_ahead, adj=True, acc=acc)
+            u_row = adj_row(n_back, i)
+            v = row_times(u_row, gm_back)
+            v = row_times(adj_row(gn_back, i), m_back, acc=v)
+            acc = row_times(v, n_diag, acc=acc)
+            v = row_times(u_row, m_back)
+            put(m, x, i, row_times(v, gn_diag, acc=acc))
+
+    build_g(2)
+    planes(2, force)
+    for copy in second_y:
+        copy.wait()
+    widen_faces((lym, hym, gym), (lyp, hyp, gyp))
+    build_g(1)
+    planes(1, force)
+    for copy in second_x:
+        copy.wait()
+    widen_faces((lxm, hxm, gxm), (lxp, hxp, gxp))
     widen_halo(lcxy, cxy, gcxy)
     widen_halo(lcyx, cyx, gcyx)
-
-    build(gown, gplus, gminus, gdiag, gxm, gxp, gym, gyp, gcxy, gcyx, False)
-
-    def force(q, _):
-        m, x = q // wx, lax.rem(q, wx)
-        base = link(cst, m, x)
-        rows_out = [row_of(base, i) for i in range(3)]
-        for k in range(1, 4):
-            n = lax.rem(m + k, 4)
-            n_own, m_ahead, n_ahead = link(own, n, x), link(plus, m, n, x), link(plus, n, m, x)
-            n_back, m_back, n_diag = link(minus, n, n, x), link(minus, m, n, x), link(diag, n, m, x)
-            gn_own, gm_ahead, gn_ahead = link(gown, n, x), link(gplus, m, n, x), link(gplus, n, m, x)
-            gn_back, gm_back, gn_diag = link(gminus, n, n, x), link(gminus, m, n, x), link(gdiag, n, m, x)
-            for i in range(3):
-                u_row = row_of(n_own, i)
-                v = row_times(u_row, gm_ahead)
-                v = row_times(row_of(gn_own, i), m_ahead, acc=v)
-                acc = row_times(v, n_ahead, adj=True, acc=rows_out[i])
-                v = row_times(u_row, m_ahead)
-                acc = row_times(v, gn_ahead, adj=True, acc=acc)
-                u_row = adj_row(n_back, i)
-                v = row_times(u_row, gm_back)
-                v = row_times(adj_row(gn_back, i), m_back, acc=v)
-                acc = row_times(v, n_diag, acc=acc)
-                v = row_times(u_row, m_back)
-                rows_out[i] = row_times(v, gn_diag, acc=acc)
-        for i in range(3):
-            for j in range(3):
-                for part in range(2):
-                    v = rows_out[i][j][part]
-                    for y in range(wy):
-                        out[m, re(i, j) + part, x, y] = v[y * ts:(y + 1) * ts, :]
+    build_g(0)
+    planes(0, force)
+
+    def deliver(c, _):
+        for d in range(4):
+            for x in range(wx):
+                for y in range(wy):
+                    out[d, c, x, y] = cst[d, c, x, y * ts:(y + 1) * ts, :]
         return 0
 
-    lax.fori_loop(0, 4 * wx, force, 0)
+    lax.fori_loop(0, COMP, deliver, 0)
 
 
 def solution(mesh):
@@ -515,15 +565,16 @@
         field = vm(dirs, COMP, wx, rows)
         pairs = vm(dirs, dirs, COMP, wx, rows)
         halo = vm(dirs, COMP, rows)
-        corner = vm(COMP, rows)
+        corner = vm(COMP, ts)
         scratch = [field, pairs, pairs, pairs, field, pairs, pairs, pairs]
         scratch += [field, field, vm(dirs, ALG, wx, rows)]
         scratch += [halo] * 4 + [corner] * 2
+        scratch += [vm(SENT, ts)] * 2 + [vm(ALG, ts)] * 2
         scratch += [vm(SENT, wy)] * 2 + [vm(SENT, wx)] * 2 + [vm(COMP, wy)] * 2 + [vm(COMP, wx)] * 2
         scratch += [vm(dirs, SENT, rows)] * 2 + [vm(dirs, ALG, rows)] * 2
-        scratch += [vm(dirs, ALG, rows)] * 4 + [vm(ALG, rows)] * 2
+        scratch += [vm(dirs, ALG, rows)] * 4 + [vm(ALG, ts)] * 2
         scratch += [halo] * 4 + [corner] * 2
-        scratch += [pltpu.SemaphoreType.DMA((16,)), pltpu.SemaphoreType.DMA((16,))]
+        scratch += [pltpu.SemaphoreType.DMA((26,)), pltpu.SemaphoreType.DMA((26,))]
         result = pl.pallas_call(
             partial(kernel, sizes),
             out_shape=jax.ShapeDtypeStruct(flat_in.shape, f32),

time: 49.1 us -> 41.5 us (0.85)
  Pallas kernels: 44.6 us -> 36.9 us
    pallas_call x1, Pallas kernels: 44.6 us -> 36.9 us  [body(): pl.pallas_call(partial(kernel, sizes), out_shape=jax.ShapeDtypeStruct(fla...]
where the time goes in v1:
time: 41.5 us; the launch traced here: 41.2 us
  Pallas kernels  36.9 us (89%)
  local copies, waits for them, and re-layouts  4.3 us (10%)
    pallas_call x1, Pallas kernels, body(): pl.pallas_call(partial(kernel, sizes), out_shape=jax.ShapeDtypeStruct(fla...  36.9 us
    unnamed x2, local copies, waits for them, and re-layouts  4.3 us

profile of v1, /device:TPU:0, one launch (start us, length us, event | category | flops | bytes accessed | tf_op | source)
XLA Modules:
  0.0 41.2 jit_solution(14005395949840185426)
XLA Ops:
  0.0 2.3 %copy.3 = f32[4,3,3,2,2,2,6,128]{7,6,5,4,3,2,1,0:T(8,128)} copy(f32[4,3,3,2,2,2,6,128]{7,5,6,4,3,2,1,0:T(2,128)} %param.2) | data formatting | bytes 1769472 | tf_op args[0]
  2.4 36.9 %stout.1 = f32[4,18,2,2,4,128]{5,4,3,2,1,0:T(4,128)} custom-call(f32[4,18,2,2,6,128]{5,4,3,2,1,0:T(8,128)} %bitcast.3, f32[4,18,2,2,4,128]{5,4,3,2,1,0:T(4,128)} %bitcast.5), custom_call_target="tpu_custom_call" | custom-call | tf_op jit(solution)/shard_map/stout/pallas_call | solution.py:578
  39.3 2.0 %copy.5 = f32[4,3,3,2,2,2,4,128]{7,6,5,4,3,2,1,0:T(4,128)} copy(f32[4,3,3,2,2,2,4,128]{7,6,5,4,3,2,1,0:T(4,128)} %bitcast.4) | data formatting | bytes 1179648
